TPU v7x, 32 devices: a whole 2x2x4 slice. The times are simulated.
32 devices in a mesh: slab: 4 (over y, x), dom: 8 (over z, core).
Axes of the slice: x: 2, y: 2, z: 4, core: 2. Of those that a mesh axis runs over, the one named last changes fastest.
Arguments:
- tiles: bfloat16 [2560, 128, 128], P('dom'), may hold values from -0.09375 to 0.09375
- volume: float32 [256, 128, 128], P(('slab', 'dom')), parts along dimension 0, may hold values from 0 to 2
- tile_voxel: int32 [2560], P('dom'), may hold values from 0 to 7
- tile_dest: int32 [2560], P('dom'), may hold values from 0 to 7
- slot_block: int32 [8, 8], P('dom'), may hold values from 0 to 7
- tile_count: int32 [8], P('dom'), may hold values from 80 to 320, as said below
- counts: int32 [256, 128, 128], P(('slab', 'dom')), parts along dimension 0, may hold values from 2000 to 29999
Outputs:
- updated: float32 [256, 128, 128], P(('slab', 'dom')), parts along dimension 0
- residual: bfloat16 [256, 128, 128], P(('slab', 'dom')), parts along dimension 0
There are 4 independent parts, one for each index of `slab`. A program takes and returns all parts, laid end to end along the dimension named above; an argument that names none is the same for every part. Nothing has to cross between parts.
Inputs may be any that keep to these rules, and one draw needn't show every extreme that they name: `tile_count`: every device holds at least max(80, 3) live tiles; some device holds 320.
All inputs are finite; a program needn't handle non-finite values.
Results may differ from a plain program's by a relative error of at most 0.006.
Values may be sent and summed in bfloat16 or wider, within the bound.
A program may use at most 128 MiB of HBM per device.

v0:
```python
import jax
import jax.numpy as jnp
from jax import lax
from jax.sharding import PartitionSpec as P

flux = 32768.0
step_size = 0.5


def on_device(tiles, volume, tile_voxel, tile_dest, slot_block, tile_count, counts):
    peer_count = lax.axis_size("dom")
    tile_slots = tiles.shape[0]
    voxel_blocks = volume.shape[0]
    owned_blocks = counts.shape[0]
    tile_rows = tiles.shape[1]
    slice_count = volume.shape[2]
    alive_mask = jnp.arange(tile_slots, dtype=jnp.int32) < tile_count[0]
    voxels_low = volume.astype(jnp.bfloat16)
    picked = voxels_low[tile_voxel]
    products = jnp.einsum("tab,tbs->tas", tiles, picked, preferred_element_type=jnp.float32)
    dest_index = jnp.where(alive_mask, tile_dest, peer_count)
    outgoing = (
        jnp.zeros((peer_count, tile_rows, slice_count), jnp.float32)
        .at[dest_index]
        .add(products, mode="drop")
    )
    incoming = lax.all_to_all(
        outgoing.astype(jnp.bfloat16), "dom", split_axis=0, concat_axis=0, tiled=True
    ).astype(outgoing.dtype)
    sinogram = (
        jnp.zeros((owned_blocks, tile_rows, slice_count), jnp.float32)
        .at[slot_block[0]]
        .add(incoming)
    )
    measured = jnp.log(flux / counts.astype(jnp.float32))
    residual = (sinogram - measured).astype(jnp.bfloat16)
    answers = residual[slot_block[0]]
    returned = lax.all_to_all(answers, "dom", split_axis=0, concat_axis=0, tiled=True)
    fetched = returned[tile_dest]
    back_products = jnp.einsum("tab,tas->tbs", tiles, fetched, preferred_element_type=jnp.float32)
    voxel_target = jnp.where(alive_mask, tile_voxel, voxel_blocks)
    gradient = (
        jnp.zeros((voxel_blocks, tile_rows, slice_count), jnp.float32)
        .at[voxel_target]
        .add(back_products, mode="drop")
    )
    updated = jnp.maximum(volume - step_size * gradient, 0.0)
    return (updated, residual)


def solution(mesh):
    in_specs = (
        P("dom", None, None),
        P(("slab", "dom"), None, None),
        P("dom"),
        P("dom"),
        P("dom", None),
        P("dom"),
        P(("slab", "dom"), None, None),
    )
    out_specs = (P(("slab", "dom"), None, None), P(("slab", "dom"), None, None))
    return jax.shard_map(
        on_device, mesh=mesh, in_specs=in_specs, out_specs=out_specs, check_vma=False
    )
```

profile of v0, /device:TPU:0, one launch (start us, length us, event | category | flops | bytes accessed | tf_op | source)
XLA Modules:
  0.0 212.2 jit_solution(15133742452892479456)
XLA Ops:
  1.3 0.7 compare_select_fusion
  2.0 1.1 convert_element_type.15
  3.1 10.7 %gather_fusion = bf16[320,128,128]{2,1,0:T(8,128)(2,1)} fusion(bf16[8,128,128]{2,1,0:T(8,128)(2,1)S(1)} %convert_element_type.15, s32[1024]{0:T(1024)S(1)} %pad_clamp_fusion.2), kind=kCustom, calls=%fused_computation | custom fusion | bytes 20972800 | tf_op jit(solution)/shard_map/gather | solution.py:19
  13.7 15.5 %convolution_bitcast_fusion.1 = f32[320,128,128]{1,2,0:T(8,128)} fusion(bf16[320,128,128]{2,1,0:T(8,128)(2,1)} %gather_fusion, bf16[320,128,128]{2,1,0:T(8,128)(2,1)} %param.7), kind=kOutput, calls=%fused_computation.7 | convolution fusion | flops 1342177280 | bytes 41943040 | tf_op jit(solution)/shard_map/tab,tbs->tas/dot_general | solution.py:20
  29.2 21.1 %copy.10 = f32[320,128,128]{2,1,0:T(8,128)} copy(f32[320,128,128]{1,2,0:T(8,128)} %convolution_bitcast_fusion.1) | data formatting | bytes 41943040 | tf_op jit(solution)/shard_map/tab,tbs->tas/dot_general | solution.py:20
  50.4 0.0 copy-start.3
  50.4 0.0 copy-start.2
  50.4 41.8 %scatter_fusion = f32[8,128,128]{2,1,0:T(8,128)S(1)} fusion(f32[8,128,128]{2,1,0:T(8,128)S(1)} %broadcast.27.clone.1, s32[320]{0:T(512)S(1)} %get-tuple-element.3, f32[320,128,128]{2,1,0:T(8,128)} %copy.10), kind=kCustom, calls=%fused_computation.3 | custom fusion | flops 5242880 | bytes 62915840 | tf_op jit(solution)/shard_map/scatter-add | solution.py:25
  92.2 0.7 convert_element_type.16
  93.0 6.4 %all-to-all-start = ((bf16[8,128,128]{2,1,0:T(8,128)(2,1)}), bf16[8,128,128]{2,1,0:T(8,128)(2,1)S(1)}, u32[]{:S(2)}, u32[]{:S(2)}) async-start(bf16[8,128,128]{2,1,0:T(8,128)(2,1)} %convert_element_type.16), calls=%async_computation | async-start | bytes 524288 | tf_op jit(solution)/shard_map/all_to_all | solution.py:27
  99.4 0.0 copy-done.3
  99.4 9.7 %all-to-all-done = bf16[8,128,128]{2,1,0:T(8,128)(2,1)S(1)} async-done(((bf16[8,128,128]{2,1,0:T(8,128)(2,1)}), bf16[8,128,128]{2,1,0:T(8,128)(2,1)S(1)}, u32[]{:S(2)}, u32[]{:S(2)}) %all-to-all-start) | async-done | bytes 262176 | tf_op jit(solution)/shard_map/all_to_all | solution.py:27
  109.2 1.0 scatter_fusion.1
  110.2 0.0 copy-done.2
  110.2 0.1 subtract_convert_fusion
  110.4 0.0 copy-start.1
  110.4 1.3 gather_fusion.1
  111.7 3.6 %all-to-all-start.1 = ((bf16[8,128,128]{2,1,0:T(8,128)(2,1)}), bf16[8,128,128]{2,1,0:T(8,128)(2,1)S(1)}, u32[]{:S(2)}, u32[]{:S(2)}) async-start(bf16[8,128,128]{2,1,0:T(8,128)(2,1)} %gather_fusion.1), calls=%async_computation.1 | async-start | bytes 524288 | tf_op jit(solution)/shard_map/all_to_all | solution.py:38
  115.3 9.4 %all-to-all-done.1 = bf16[8,128,128]{2,1,0:T(8,128)(2,1)S(1)} async-done(((bf16[8,128,128]{2,1,0:T(8,128)(2,1)}), bf16[8,128,128]{2,1,0:T(8,128)(2,1)S(1)}, u32[]{:S(2)}, u32[]{:S(2)}) %all-to-all-start.1) | async-done | bytes 262176 | tf_op jit(solution)/shard_map/all_to_all | solution.py:38
  124.8 10.6 %gather_fusion.2 = bf16[320,128,128]{2,1,0:T(8,128)(2,1)} fusion(bf16[8,128,128]{2,1,0:T(8,128)(2,1)S(1)} %all-to-all-done.1, s32[1024]{0:T(1024)S(1)} %pad_clamp_fusion), kind=kCustom, calls=%fused_computation.2 | custom fusion | bytes 20972800 | tf_op jit(solution)/shard_map/gather | solution.py:39
  135.4 0.0 copy-done.1
  135.4 12.9 %convolution_bitcast_fusion = f32[320,128,128]{1,2,0:T(8,128)} fusion(bf16[320,128,128]{2,1,0:T(8,128)(2,1)} %gather_fusion.2, bf16[320,128,128]{2,1,0:T(8,128)(2,1)} %param.7), kind=kOutput, calls=%fused_computation.6 | convolution fusion | flops 1342177280 | bytes 41943040 | tf_op jit(solution)/shard_map/tab,tas->tbs/dot_general | solution.py:40
  148.3 21.1 %copy.12 = f32[320,128,128]{2,1,0:T(8,128)} copy(f32[320,128,128]{1,2,0:T(8,128)} %convolution_bitcast_fusion) | data formatting | bytes 41943040 | tf_op jit(solution)/shard_map/tab,tas->tbs/dot_general | solution.py:40
  169.5 0.0 copy-start
  169.5 41.8 %scatter_fusion.2 = f32[8,128,128]{2,1,0:T(8,128)S(1)} fusion(f32[8,128,128]{2,1,0:T(8,128)S(1)} %broadcast.27, s32[320]{0:T(512)S(1)} %get-tuple-element.6, f32[320,128,128]{2,1,0:T(8,128)} %copy.12), kind=kCustom, calls=%fused_computation.5 | custom fusion | flops 5242880 | bytes 62915840 | tf_op jit(solution)/shard_map/scatter-add | solution.py:45
  211.3 0.0 copy-done
  211.3 0.9 subtract_maximum_fusion
  (8 shorter events, 0.2 us)
Async XLA Ops:
  50.4 49.0 %copy-start.3 = (s32[1,8]{1,0:T(1,128)S(1)}, s32[1,8]{1,0:T(1,128)}, u32[]{:S(2)}) copy-start(s32[1,8]{1,0:T(1,128)} %param.11) | copy-start | bytes 100
  50.4 59.8 %copy-start.2 = (s32[8,128,128]{2,1,0:T(8,128)S(1)}, s32[8,128,128]{2,1,0:T(8,128)}, u32[]{:S(2)}) copy-start(s32[8,128,128]{2,1,0:T(8,128)} %param.13) | copy-start | bytes 1572868
  93.0 16.1 %all-to-all-start = ((bf16[8,128,128]{2,1,0:T(8,128)(2,1)}), bf16[8,128,128]{2,1,0:T(8,128)(2,1)S(1)}, u32[]{:S(2)}, u32[]{:S(2)}) async-start(bf16[8,128,128]{2,1,0:T(8,128)(2,1)} %convert_element_type.16), calls=%async_computation | async-start | bytes 524288 | tf_op jit(solution)/shard_map/all_to_all | solution.py:27
  110.4 25.0 %copy-start.1 = (bf16[8,128,128]{2,1,0:T(8,128)(2,1)}, bf16[8,128,128]{2,1,0:T(8,128)(2,1)S(1)}, u32[]{:S(2)}) copy-start(bf16[8,128,128]{2,1,0:T(8,128)(2,1)S(1)} %subtract_convert_fusion) | copy-start | bytes 786436
  111.7 13.1 %all-to-all-start.1 = ((bf16[8,128,128]{2,1,0:T(8,128)(2,1)}), bf16[8,128,128]{2,1,0:T(8,128)(2,1)S(1)}, u32[]{:S(2)}, u32[]{:S(2)}) async-start(bf16[8,128,128]{2,1,0:T(8,128)(2,1)} %gather_fusion.1), calls=%async_computation.1 | async-start | bytes 524288 | tf_op jit(solution)/shard_map/all_to_all | solution.py:38
  169.5 41.9 %copy-start = (f32[8,128,128]{2,1,0:T(8,128)S(1)}, f32[8,128,128]{2,1,0:T(8,128)}, u32[]{:S(2)}) copy-start(f32[8,128,128]{2,1,0:T(8,128)} %param.8) | copy-start | bytes 1572868
where the time goes:
time: 215 us; the launch traced here: 212 us
  other arithmetic  88.3 us (41%)
  local copies, waits for them, and re-layouts  64.9 us (30%)
  matrix products  28.4 us (13%)
  waiting for transfers between devices  19.1 us (9%)
  starting transfers between devices  10 us (5%)
    scatter-add x1, other arithmetic, on_device(): gradient = jnp.zeros((voxel_blocks, tile_rows, slice_count), jnp.float32)...  41.8 us
    scatter-add x1, other arithmetic, on_device(): outgoing = jnp.zeros((peer_count, tile_rows, slice_count), jnp.float32).a...  41.8 us
    dot_general x1, local copies, waits for them, and re-layouts, on_device(): jnp.einsum('tab,tas->tbs', tiles, fetched, preferred_element_type=jnp.flo...  21.1 us
    dot_general x1, local copies, waits for them, and re-layouts, on_device(): jnp.einsum('tab,tbs->tas', tiles, picked, preferred_element_type=jnp.floa...  21.1 us
    dot_general x1, matrix products, on_device(): jnp.einsum('tab,tbs->tas', tiles, picked, preferred_element_type=jnp.floa...  15.5 us
    dot_general x1, matrix products, on_device(): jnp.einsum('tab,tas->tbs', tiles, fetched, preferred_element_type=jnp.flo...  12.9 us
    gather x1, local copies, waits for them, and re-layouts, on_device(): picked = voxels_low[tile_voxel]  10.7 us
    gather x1, local copies, waits for them, and re-layouts, on_device(): fetched = returned[tile_dest]  10.6 us
  transfers between devices with their start and end apart: 2, of which 2 were waited for; matrix products, arithmetic and copies ran while one was open for 0% of the time, Pallas kernels for 0%

commit v1 on v0

v1 whole, which is shorter than its diff:
```python
import functools

import jax
import jax.numpy as jnp
from jax import lax
from jax.experimental import pallas as pl
from jax.experimental.pallas import tpu as pltpu
from jax.sharding import PartitionSpec as P

flux = 32768.0
step_size = 0.5
GROUP = 16
PARTS = 4
PHASES = 2
VMEM_BUDGET = 40 * 1024 * 1024


def fold_kernel(voxel_blocks, dest_ref, voxel_ref, count_ref, tiles_ref, w_ref, tile_buf, sems, *acc):
    slots, rows, cols = tile_buf.shape
    groups = slots // GROUP
    part = rows // PARTS
    count = count_ref[0]

    def fetch(g):
        at = pl.ds(g * GROUP, GROUP)
        return pltpu.make_async_copy(tiles_ref.at[at], tile_buf.at[at], sems.at[g])

    for g in range(groups):
        @pl.when(g * GROUP < count)
        def _(g=g):
            fetch(g).start()

    for a in acc:
        a[...] = jnp.zeros_like(a)

    def add_tile(i):
        bucket = dest_ref[i] * voxel_blocks + voxel_ref[i]
        for q, a in enumerate(acc):
            a[bucket] += tile_buf[i, q * part:(q + 1) * part, :].astype(jnp.float32)

    @pl.loop(0, groups)
    def _(g):
        live = jnp.clip(count - g * GROUP, 0, GROUP)

        @pl.when(live > 0)
        def _():
            fetch(g).wait()

        @pl.when(live == GROUP)
        def _():
            for j in range(GROUP):
                add_tile(g * GROUP + j)

        @pl.when(live < GROUP)
        def _():
            @pl.loop(0, live)
            def _(j):
                add_tile(g * GROUP + j)

    peers = w_ref.shape[0] // rows

    @pl.loop(0, peers)
    def _(d):
        for v in range(voxel_blocks):
            for q, a in enumerate(acc):
                w_ref[pl.ds(pl.multiple_of(d * rows + q * part, part), part), v * cols:(v + 1) * cols] = (
                    a[d * voxel_blocks + v].astype(jnp.bfloat16))


def peer_order(n, me):
    chips = n // 2
    z, core = me // 2, me % 2
    sign = 1 - 2 * (z % 2)
    hops = sorted(range(1, chips), key=lambda k: (abs(2 * k - chips), k))
    order = []
    for k in hops:
        there = (z - sign * k + chips) % chips
        order += [there * 2 + core, there * 2 + 1 - core]
    return order + [z * 2 + 1 - core]


def exchange_kernel(n, slot_ref, w_ref, volume_ref, counts_ref, updated_ref, residual_ref,
                    out_buf, in_buf, answer_buf, back_buf, low, measured, grad,
                    out_send, out_recv, back_send, back_recv):
    me = lax.axis_index("dom")
    blocks, rows, lanes = volume_ref.shape
    owned = counts_ref.shape[0]
    step = rows // PHASES
    order = peer_order(n, me)

    barrier = pltpu.get_barrier_semaphore()
    for peer in order:
        pl.semaphore_signal(barrier, inc=1, device_id={"dom": peer}, device_id_type=pl.DeviceIdType.MESH)

    for v in range(blocks):
        low[v * rows:(v + 1) * rows, :] = volume_ref[v].astype(jnp.bfloat16)

    def project(d, p):
        at = pl.ds(pl.multiple_of(d * rows + p * step, step), step)
        return jnp.dot(w_ref[at, :], low[...], preferred_element_type=jnp.float32).astype(jnp.bfloat16)

    def send(src, dst, send_sems, recv_sems, peer, p):
        return pltpu.make_async_remote_copy(
            src_ref=src.at[peer, p], dst_ref=dst.at[me, p],
            send_sem=send_sems.at[peer, p], recv_sem=recv_sems.at[me, p],
            device_id={"dom": peer}, device_id_type=pl.DeviceIdType.MESH)

    def arrival(dst, send_sems, recv_sems, peer, p):
        return pltpu.make_async_remote_copy(
            src_ref=dst.at[peer, p], dst_ref=dst.at[peer, p],
            send_sem=send_sems.at[peer, p], recv_sem=recv_sems.at[peer, p],
            device_id={"dom": peer}, device_id_type=pl.DeviceIdType.MESH)

    first = True
    for p in range(PHASES):
        for peer in order:
            out_buf[peer, p] = project(peer, p)
            if first:
                pl.semaphore_wait(barrier, n - 1)
                first = False
            send(out_buf, in_buf, out_send, out_recv, peer, p).start()
    for p in range(PHASES):
        in_buf[me, p] = project(me, p)
    for b in range(owned):
        measured[b] = jnp.log(flux / counts_ref[b].astype(jnp.float32))

    for p in range(PHASES):
        for peer in reversed(order):
            arrival(in_buf, out_send, out_recv, peer, p).wait_recv()
        at = slice(p * step, (p + 1) * step)
        for b in range(owned):
            total = jnp.zeros((step, lanes), jnp.float32)
            for s in range(n):
                total += jnp.where(slot_ref[0, s] == b, in_buf[s, p].astype(jnp.float32), 0.0)
            residual_ref[b, at, :] = (total - measured[b, at, :]).astype(jnp.bfloat16)
        for peer in order:
            answer_buf[peer, p] = residual_ref[slot_ref[0, peer], at, :]
            send(answer_buf, back_buf, back_send, back_recv, peer, p).start()
        back_buf[me, p] = residual_ref[slot_ref[0, me], at, :]

    def pull(d):
        held = back_buf[d].reshape(rows, lanes)
        at = pl.ds(pl.multiple_of(d * rows, rows), rows)
        return jnp.dot(held.T, w_ref[at, :], preferred_element_type=jnp.float32)

    grad[...] = pull(me)
    for peer in reversed(order):
        for p in range(PHASES):
            arrival(back_buf, back_send, back_recv, peer, p).wait_recv()
        grad[...] += pull(peer)
    for v in range(blocks):
        updated_ref[v] = jnp.maximum(
            volume_ref[v] - step_size * grad[:, v * rows:(v + 1) * rows].T, 0.0)
    for p in range(PHASES):
        for peer in order:
            send(out_buf, in_buf, out_send, out_recv, peer, p).wait_send()
            send(answer_buf, back_buf, back_send, back_recv, peer, p).wait_send()


def fused(tiles, volume, tile_voxel, tile_dest, slot_block, tile_count, counts):
    n = lax.axis_size("dom")
    slots, rows, cols = tiles.shape
    blocks, _, lanes = volume.shape
    smem = pl.BlockSpec(memory_space=pltpu.SMEM)
    vmem = pl.BlockSpec(memory_space=pltpu.VMEM)
    anywhere = pl.BlockSpec(memory_space=pl.ANY)
    weights = pl.pallas_call(
        functools.partial(fold_kernel, blocks),
        out_shape=jax.ShapeDtypeStruct((n * rows, blocks * cols), jnp.bfloat16),
        in_specs=[smem, smem, smem, anywhere],
        out_specs=vmem,
        scratch_shapes=[
            pltpu.VMEM(tiles.shape, tiles.dtype),
            pltpu.SemaphoreType.DMA((slots // GROUP,)),
        ] + [pltpu.VMEM((n * blocks, rows // PARTS, cols), jnp.float32)] * PARTS,
        name="fold_tiles",
    )(tile_dest, tile_voxel, tile_count, tiles)

    split = (n, PHASES, rows // PHASES, lanes)
    updated, residual = pl.pallas_call(
        functools.partial(exchange_kernel, n),
        out_shape=(
            jax.ShapeDtypeStruct(volume.shape, jnp.float32),
            jax.ShapeDtypeStruct(counts.shape, jnp.bfloat16),
        ),
        in_specs=[smem, vmem, vmem, vmem],
        out_specs=(vmem, vmem),
        scratch_shapes=[pltpu.VMEM(split, jnp.bfloat16)] * 4 + [
            pltpu.VMEM((blocks * rows, lanes), jnp.bfloat16),
            pltpu.VMEM(counts.shape, jnp.float32),
            pltpu.VMEM((lanes, blocks * rows), jnp.float32),
        ] + [pltpu.SemaphoreType.DMA((n, PHASES))] * 4,
        compiler_params=pltpu.CompilerParams(collective_id=0, has_side_effects=True),
        name="exchange",
    )(slot_block, weights, volume, counts)
    return updated, residual


def general(tiles, volume, tile_voxel, tile_dest, slot_block, tile_count, counts):
    peer_count = lax.axis_size("dom")
    tile_slots, tile_rows = tiles.shape[:2]
    voxel_blocks, _, slice_count = volume.shape
    alive = jnp.arange(tile_slots, dtype=jnp.int32) < tile_count[0]
    picked = volume.astype(jnp.bfloat16)[tile_voxel]
    products = jnp.einsum("tab,tbs->tas", tiles, picked, preferred_element_type=jnp.float32)
    outgoing = (
        jnp.zeros((peer_count, tile_rows, slice_count), jnp.float32)
        .at[jnp.where(alive, tile_dest, peer_count)]
        .add(products, mode="drop")
    )
    incoming = lax.all_to_all(
        outgoing.astype(jnp.bfloat16), "dom", split_axis=0, concat_axis=0, tiled=True
    ).astype(jnp.float32)
    sinogram = jnp.zeros(counts.shape, jnp.float32).at[slot_block[0]].add(incoming)
    measured = jnp.log(flux / counts.astype(jnp.float32))
    residual = (sinogram - measured).astype(jnp.bfloat16)
    returned = lax.all_to_all(residual[slot_block[0]], "dom", split_axis=0, concat_axis=0, tiled=True)
    back = jnp.einsum("tab,tas->tbs", tiles, returned[tile_dest], preferred_element_type=jnp.float32)
    gradient = (
        jnp.zeros(volume.shape, jnp.float32)
        .at[jnp.where(alive, tile_voxel, voxel_blocks)]
        .add(back, mode="drop")
    )
    return jnp.maximum(volume - step_size * gradient, 0.0), residual


def on_device(tiles, volume, *rest):
    n = lax.axis_size("dom")
    need = tiles.size * 2 + n * volume.shape[0] * tiles.shape[1] * tiles.shape[2] * 6
    if need > VMEM_BUDGET or n % 2 or tiles.shape[0] % GROUP:
        return general(tiles, volume, *rest)
    return fused(tiles, volume, *rest)


def solution(mesh):
    both = P(("slab", "dom"), None, None)
    in_specs = (P("dom", None, None), both, P("dom"), P("dom"), P("dom", None), P("dom"), both)
    return jax.shard_map(on_device, mesh=mesh, in_specs=in_specs, out_specs=(both, both), check_vma=False)
```

time: 215 us -> 33.2 us (0.15); the launches traced: 212 us -> 33.2 us
  other arithmetic: 88.3 us -> 0 us
  local copies, waits for them, and re-layouts: 64.9 us -> 3.54 us
  matrix products: 28.4 us -> 0 us
  Pallas kernels: 0 us -> 28.4 us
  waiting for transfers between devices: 19.1 us -> 0 us
  starting transfers between devices: 10 us -> 0 us
    scatter-add x3 -> x0, other arithmetic: 84.7 us -> none  [the longest x1 41.8 us: on_device(): gradient = jnp.zeros((voxel_blocks, tile_rows, slice_count), jnp.float32)...]
    dot_general x2 -> x0, local copies, waits for them, and re-layouts: 42.2 us -> none  [the longest x1 21.1 us: on_device(): jnp.einsum('tab,tas->tbs', tiles, fetched, preferred_element_type=jnp.flo...]
    dot_general x2 -> x0, matrix products: 28.4 us -> none  [the longest x1 15.5 us: on_device(): jnp.einsum('tab,tbs->tas', tiles, picked, preferred_element_type=jnp.floa...]
    pallas_call x0 -> x2, Pallas kernels: none -> 28.4 us  [the longest x1 23.4 us: fused(): pl.pallas_call(functools.partial(exchange_kernel, n), out_shape=(jax.Shap...]
    gather x3 -> x0, local copies, waits for them, and re-layouts: 22.6 us -> none  [the longest x1 10.7 us: on_device(): picked = voxels_low[tile_voxel]]
    all_to_all x2 -> x0, waiting for transfers between devices: 19.1 us -> none  [the longest x1 9.68 us: on_device(): lax.all_to_all(outgoing.astype(jnp.bfloat16), 'dom', split_axis=0, concat...]
    all_to_all x2 -> x0, starting transfers between devices: 10 us -> none  [the longest x1 6.42 us: on_device(): lax.all_to_all(outgoing.astype(jnp.bfloat16), 'dom', split_axis=0, concat...]
    unnamed x8 -> x2, local copies, waits for them, and re-layouts: 0.03 us -> 3.54 us
  transfers between devices with their start and end apart: 2 -> 0, of which waited for: 2 -> 0; matrix products, arithmetic and copies ran while one was open for 0% -> 0% of each run, Pallas kernels for 0% -> 0%
where the time goes in v1:
time: 33.2 us
  Pallas kernels  28.4 us (86%)
  local copies, waits for them, and re-layouts  3.54 us (11%)
  between operations  1.29 us (4%)
    pallas_call x1, Pallas kernels, fused(): pl.pallas_call(functools.partial(exchange_kernel, n), out_shape=(jax.Shap...  23.4 us
    pallas_call x1, Pallas kernels, fused(): pl.pallas_call(functools.partial(fold_kernel, blocks), out_shape=jax.Shap...  4.93 us
    unnamed x2, local copies, waits for them, and re-layouts  3.54 us

profile of v1, /device:TPU:0, one launch (start us, length us, event | category | flops | bytes accessed | tf_op | source)
XLA Modules:
  0.0 33.2 jit_solution(2286563694855216115)
XLA Ops:
  1.3 4.9 %fold_tiles.1.w_ref = bf16[1024,1024]{1,0:T(8,128)(2,1)} custom-call(s32[320]{0:T(512)} %dest_ref.1, s32[320]{0:T(512)} %voxel_ref.1, s32[1]{0:T(128)S(6)} %copy.11.count_ref, bf16[320,128,128]{2,1,0:T(8,128)(2,1)} %tiles_ref.1), custom_call_target="tpu_custom_call" | custom-call | tf_op jit(solution)/shard_map/fold_tiles/pallas_call | solution.py:167
  6.2 23.4 %exchange.1 = (f32[8,128,128]{2,1,0:T(8,128)}, bf16[8,128,128]{2,1,0:T(8,128)(2,1)}) custom-call(s32[1,8]{1,0:T(1,128)} %slot_ref.1, bf16[1024,1024]{1,0:T(8,128)(2,1)} %fold_tiles.1.w_ref, f32[8,128,128]{2,1,0:T(8,128)} %volume_ref.1, s32[8,128,128]{2,1,0:T(8,128)} %counts_ref.1), custom_call_target="tpu_custom_call" | custom-call | tf_op jit(solution)/shard_map/exchange/pallas_call | solution.py:180
  29.7 1.9 %copy.12 = f32[8,128,128]{2,1,0:T(8,128)} copy(f32[8,128,128]{2,1,0:T(8,128)} %get-tuple-element.4) | data formatting | bytes 1048576
  31.5 1.7 %copy.13 = bf16[8,128,128]{2,1,0:T(8,128)(2,1)} copy(bf16[8,128,128]{2,1,0:T(8,128)(2,1)} %get-tuple-element.5) | data formatting | bytes 524288

commit v2 on v1

--- a/solution.py
+++ b/solution.py
@@ -12,26 +12,36 @@
 GROUP = 16
 PARTS = 4
 PHASES = 2
-VMEM_BUDGET = 40 * 1024 * 1024
-
-
-def fold_kernel(voxel_blocks, dest_ref, voxel_ref, count_ref, tiles_ref, w_ref, tile_buf, sems, *acc):
+FOLD_VMEM = 57 * 1024 * 1024
+EXCHANGE_VMEM = 10 * 1024 * 1024
+VMEM_BUDGET = 18 * 1024 * 1024
+
+
+def fold_kernel(voxel_blocks, dest_hbm, voxel_hbm, count_hbm, tiles_ref, w_ref,
+                dest_ref, voxel_ref, count_ref, tile_buf, table_sems, sems, *acc):
     slots, rows, cols = tile_buf.shape
     groups = slots // GROUP
     part = rows // PARTS
-    count = count_ref[0]
+    tables = [
+        pltpu.make_async_copy(src, dst, table_sems.at[i])
+        for i, (src, dst) in enumerate(
+            ((dest_hbm, dest_ref), (voxel_hbm, voxel_ref), (count_hbm, count_ref)))
+    ]
+    for table in tables:
+        table.start()
 
     def fetch(g):
         at = pl.ds(g * GROUP, GROUP)
         return pltpu.make_async_copy(tiles_ref.at[at], tile_buf.at[at], sems.at[g])
 
     for g in range(groups):
-        @pl.when(g * GROUP < count)
-        def _(g=g):
-            fetch(g).start()
+        fetch(g).start()
 
     for a in acc:
         a[...] = jnp.zeros_like(a)
+    for table in tables:
+        table.wait()
+    count = count_ref[0]
 
     def add_tile(i):
         bucket = dest_ref[i] * voxel_blocks + voxel_ref[i]
@@ -42,9 +52,7 @@
     def _(g):
         live = jnp.clip(count - g * GROUP, 0, GROUP)
 
-        @pl.when(live > 0)
-        def _():
-            fetch(g).wait()
+        fetch(g).wait()
 
         @pl.when(live == GROUP)
         def _():
@@ -163,16 +171,21 @@
     blocks, _, lanes = volume.shape
     smem = pl.BlockSpec(memory_space=pltpu.SMEM)
     vmem = pl.BlockSpec(memory_space=pltpu.VMEM)
-    anywhere = pl.BlockSpec(memory_space=pl.ANY)
+    hbm = pl.BlockSpec(memory_space=pltpu.HBM)
     weights = pl.pallas_call(
         functools.partial(fold_kernel, blocks),
-        out_shape=jax.ShapeDtypeStruct((n * rows, blocks * cols), jnp.bfloat16),
-        in_specs=[smem, smem, smem, anywhere],
+        out_shape=pltpu.VMEM((n * rows, blocks * cols), jnp.bfloat16),
+        in_specs=[hbm] * 4,
         out_specs=vmem,
         scratch_shapes=[
+            pltpu.SMEM(tile_dest.shape, jnp.int32),
+            pltpu.SMEM(tile_voxel.shape, jnp.int32),
+            pltpu.SMEM(tile_count.shape, jnp.int32),
             pltpu.VMEM(tiles.shape, tiles.dtype),
+            pltpu.SemaphoreType.DMA((3,)),
             pltpu.SemaphoreType.DMA((slots // GROUP,)),
         ] + [pltpu.VMEM((n * blocks, rows // PARTS, cols), jnp.float32)] * PARTS,
+        compiler_params=pltpu.CompilerParams(vmem_limit_bytes=FOLD_VMEM),
         name="fold_tiles",
     )(tile_dest, tile_voxel, tile_count, tiles)
 
@@ -190,7 +203,7 @@
             pltpu.VMEM(counts.shape, jnp.float32),
             pltpu.VMEM((lanes, blocks * rows), jnp.float32),
         ] + [pltpu.SemaphoreType.DMA((n, PHASES))] * 4,
-        compiler_params=pltpu.CompilerParams(collective_id=0, has_side_effects=True),
+        compiler_params=pltpu.CompilerParams(collective_id=0, has_side_effects=True, vmem_limit_bytes=EXCHANGE_VMEM),
         name="exchange",
     )(slot_block, weights, volume, counts)
     return updated, residual

time: 33.2 us -> 27.1 us (0.82)
  Pallas kernels: 28.4 us -> 24 us
  local copies, waits for them, and re-layouts: 3.54 us -> 1.51 us
    pallas_call x1, Pallas kernels: 23.4 us -> 19.3 us  [fused(): pl.pallas_call(functools.partial(exchange_kernel, n), out_shape=(jax.Shap...]
    unnamed x2 -> x8, local copies, waits for them, and re-layouts: 3.54 us -> 1.51 us
where the time goes in v2:
time: 27.1 us; the launch traced here: 27 us
  Pallas kernels  24 us (89%)
  local copies, waits for them, and re-layouts  1.51 us (6%)
  between operations  1.43 us (5%)
    pallas_call x1, Pallas kernels, fused(): pl.pallas_call(functools.partial(exchange_kernel, n), out_shape=(jax.Shap...  19.3 us
    pallas_call x1, Pallas kernels, fused(): pl.pallas_call(functools.partial(fold_kernel, blocks), out_shape=pltpu.VM...  4.73 us
    unnamed x8, local copies, waits for them, and re-layouts  1.51 us

profile of v2, /device:TPU:0, one launch (start us, length us, event | category | flops | bytes accessed | tf_op | source)
XLA Modules:
  0.0 27.0 jit_solution(2508743388560671245)
XLA Ops:
  0.6 0.0 copy-start.1
  0.6 0.0 copy-start.2
  0.7 0.0 copy-start
  1.4 4.7 %fold_tiles.1.w_ref = bf16[1024,1024]{1,0:T(8,128)(2,1)S(1)} custom-call(s32[320]{0:T(512)} %dest_hbm.1, s32[320]{0:T(512)} %voxel_hbm.1, s32[1]{0:T(128)S(6)} %copy.11.count_hbm, bf16[320,128,128]{2,1,0:T(8,128)(2,1)} %tiles_ref.1), custom_call_target="tpu_custom_call" | custom-call | tf_op jit(solution)/shard_map/fold_tiles/pallas_call | solution.py:175
  6.1 0.0 copy-done.1
  6.1 0.0 copy-done.2
  6.2 0.0 copy-done
  6.2 19.3 %exchange.1 = (f32[8,128,128]{2,1,0:T(8,128)S(1)}, bf16[8,128,128]{2,1,0:T(8,128)(2,1)S(1)}) custom-call(s32[1,8]{1,0:T(1,128)S(1)} %copy-done.2, bf16[1024,1024]{1,0:T(8,128)(2,1)S(1)} %fold_tiles.1.w_ref, f32[8,128,128]{2,1,0:T(8,128)S(1)} %copy-done, s32[8,128,128]{2,1,0:T(8,128)S(1)} %copy-done.1), custom_call_target="tpu_custom_call" | custom-call | tf_op jit(solution)/shard_map/exchange/pallas_call | solution.py:193
  25.5 0.8 %copy.12 = f32[8,128,128]{2,1,0:T(8,128)} copy(f32[8,128,128]{2,1,0:T(8,128)S(1)} %get-tuple-element.4) | data formatting | bytes 1048576
  26.3 0.7 %copy.13 = bf16[8,128,128]{2,1,0:T(8,128)(2,1)} copy(bf16[8,128,128]{2,1,0:T(8,128)(2,1)S(1)} %get-tuple-element.5) | data formatting | bytes 524288
Async XLA Ops:
  0.6 5.5 %copy-start.1 = (s32[8,128,128]{2,1,0:T(8,128)S(1)}, s32[8,128,128]{2,1,0:T(8,128)}, u32[]{:S(2)}) copy-start(s32[8,128,128]{2,1,0:T(8,128)} %counts_ref.1) | copy-start | bytes 1572868
  0.6 5.5 %copy-start.2 = (s32[1,8]{1,0:T(1,128)S(1)}, s32[1,8]{1,0:T(1,128)}, u32[]{:S(2)}) copy-start(s32[1,8]{1,0:T(1,128)} %slot_ref.1) | copy-start | bytes 100
  0.7 5.5 %copy-start = (f32[8,128,128]{2,1,0:T(8,128)S(1)}, f32[8,128,128]{2,1,0:T(8,128)}, u32[]{:S(2)}) copy-start(f32[8,128,128]{2,1,0:T(8,128)} %volume_ref.1) | copy-start | bytes 1572868

commit v3 on v2

--- a/solution.py
+++ b/solution.py
@@ -12,13 +12,13 @@
 GROUP = 16
 PARTS = 4
 PHASES = 2
-FOLD_VMEM = 57 * 1024 * 1024
+FOLD_VMEM = 53 * 1024 * 1024
 EXCHANGE_VMEM = 10 * 1024 * 1024
 VMEM_BUDGET = 18 * 1024 * 1024
 
 
-def fold_kernel(voxel_blocks, dest_hbm, voxel_hbm, count_hbm, tiles_ref, w_ref,
-                dest_ref, voxel_ref, count_ref, tile_buf, table_sems, sems, *acc):
+def fold_kernel(voxel_blocks, dest_hbm, voxel_hbm, count_hbm, tiles_ref, *refs):
+    acc, (dest_ref, voxel_ref, count_ref, tile_buf, table_sems, sems) = refs[:PARTS], refs[PARTS:]
     slots, rows, cols = tile_buf.shape
     groups = slots // GROUP
     part = rows // PARTS
@@ -65,15 +65,6 @@
             def _(j):
                 add_tile(g * GROUP + j)
 
-    peers = w_ref.shape[0] // rows
-
-    @pl.loop(0, peers)
-    def _(d):
-        for v in range(voxel_blocks):
-            for q, a in enumerate(acc):
-                w_ref[pl.ds(pl.multiple_of(d * rows + q * part, part), part), v * cols:(v + 1) * cols] = (
-                    a[d * voxel_blocks + v].astype(jnp.bfloat16))
-
 
 def peer_order(n, me):
     chips = n // 2
@@ -87,13 +78,15 @@
     return order + [z * 2 + 1 - core]
 
 
-def exchange_kernel(n, slot_ref, w_ref, volume_ref, counts_ref, updated_ref, residual_ref,
-                    out_buf, in_buf, answer_buf, back_buf, low, measured, grad,
-                    out_send, out_recv, back_send, back_recv):
+def exchange_kernel(n, slot_ref, volume_ref, counts_ref, *refs):
+    acc, (grad_ref, residual_ref), scratch = refs[:PARTS], refs[PARTS:PARTS + 2], refs[PARTS + 2:]
+    (out_buf, in_buf, answer_buf, landing, w_ref, low, measured,
+     out_send, out_recv, back_send, back_recv) = scratch
     me = lax.axis_index("dom")
     blocks, rows, lanes = volume_ref.shape
     owned = counts_ref.shape[0]
     step = rows // PHASES
+    part = rows // PARTS
     order = peer_order(n, me)
 
     barrier = pltpu.get_barrier_semaphore()
@@ -104,6 +97,10 @@
         low[v * rows:(v + 1) * rows, :] = volume_ref[v].astype(jnp.bfloat16)
 
     def project(d, p):
+        for q in range(p * step // part, (p + 1) * step // part):
+            at = pl.ds(pl.multiple_of(d * rows + q * part, part), part)
+            for v in range(blocks):
+                w_ref[at, v * rows:(v + 1) * rows] = acc[q][d * blocks + v].astype(jnp.bfloat16)
         at = pl.ds(pl.multiple_of(d * rows + p * step, step), step)
         return jnp.dot(w_ref[at, :], low[...], preferred_element_type=jnp.float32).astype(jnp.bfloat16)
 
@@ -143,26 +140,36 @@
             residual_ref[b, at, :] = (total - measured[b, at, :]).astype(jnp.bfloat16)
         for peer in order:
             answer_buf[peer, p] = residual_ref[slot_ref[0, peer], at, :]
-            send(answer_buf, back_buf, back_send, back_recv, peer, p).start()
-        back_buf[me, p] = residual_ref[slot_ref[0, me], at, :]
+            send(answer_buf, landing, back_send, back_recv, peer, p).start()
+        landing[me, p] = residual_ref[slot_ref[0, me], at, :]
 
     def pull(d):
-        held = back_buf[d].reshape(rows, lanes)
+        held = landing[d].reshape(rows, lanes)
         at = pl.ds(pl.multiple_of(d * rows, rows), rows)
         return jnp.dot(held.T, w_ref[at, :], preferred_element_type=jnp.float32)
 
-    grad[...] = pull(me)
+    grad_ref[...] = pull(me)
     for peer in reversed(order):
         for p in range(PHASES):
-            arrival(back_buf, back_send, back_recv, peer, p).wait_recv()
-        grad[...] += pull(peer)
-    for v in range(blocks):
-        updated_ref[v] = jnp.maximum(
-            volume_ref[v] - step_size * grad[:, v * rows:(v + 1) * rows].T, 0.0)
+            arrival(landing, back_send, back_recv, peer, p).wait_recv()
+        grad_ref[...] += pull(peer)
     for p in range(PHASES):
         for peer in order:
             send(out_buf, in_buf, out_send, out_recv, peer, p).wait_send()
-            send(answer_buf, back_buf, back_send, back_recv, peer, p).wait_send()
+            send(answer_buf, landing, back_send, back_recv, peer, p).wait_send()
+
+
+def finish_kernel(volume_ref, grad_ref, residual_ref, updated_hbm, residual_hbm, updated, sems):
+    blocks, rows, _ = volume_ref.shape
+    copies = [pltpu.make_async_copy(residual_ref, residual_hbm, sems.at[blocks])]
+    copies[0].start()
+    for v in range(blocks):
+        updated[v] = jnp.maximum(
+            volume_ref[v] - step_size * grad_ref[:, v * rows:(v + 1) * rows].T, 0.0)
+        copies.append(pltpu.make_async_copy(updated.at[v], updated_hbm.at[v], sems.at[v]))
+        copies[-1].start()
+    for copy in copies:
+        copy.wait()
 
 
 def fused(tiles, volume, tile_voxel, tile_dest, slot_block, tile_count, counts):
@@ -172,11 +179,11 @@
     smem = pl.BlockSpec(memory_space=pltpu.SMEM)
     vmem = pl.BlockSpec(memory_space=pltpu.VMEM)
     hbm = pl.BlockSpec(memory_space=pltpu.HBM)
-    weights = pl.pallas_call(
+    sums = pl.pallas_call(
         functools.partial(fold_kernel, blocks),
-        out_shape=pltpu.VMEM((n * rows, blocks * cols), jnp.bfloat16),
+        out_shape=[pltpu.VMEM((n * blocks, rows // PARTS, cols), jnp.float32)] * PARTS,
         in_specs=[hbm] * 4,
-        out_specs=vmem,
+        out_specs=[vmem] * PARTS,
         scratch_shapes=[
             pltpu.SMEM(tile_dest.shape, jnp.int32),
             pltpu.SMEM(tile_voxel.shape, jnp.int32),
@@ -184,29 +191,44 @@
             pltpu.VMEM(tiles.shape, tiles.dtype),
             pltpu.SemaphoreType.DMA((3,)),
             pltpu.SemaphoreType.DMA((slots // GROUP,)),
-        ] + [pltpu.VMEM((n * blocks, rows // PARTS, cols), jnp.float32)] * PARTS,
+        ],
         compiler_params=pltpu.CompilerParams(vmem_limit_bytes=FOLD_VMEM),
         name="fold_tiles",
     )(tile_dest, tile_voxel, tile_count, tiles)
 
     split = (n, PHASES, rows // PHASES, lanes)
-    updated, residual = pl.pallas_call(
+    gradient, residual = pl.pallas_call(
         functools.partial(exchange_kernel, n),
+        out_shape=(
+            pltpu.VMEM((lanes, blocks * cols), jnp.float32),
+            pltpu.VMEM(counts.shape, jnp.bfloat16),
+        ),
+        in_specs=[smem] + [vmem] * (2 + PARTS),
+        out_specs=(vmem, vmem),
+        scratch_shapes=[pltpu.VMEM(split, jnp.bfloat16)] * 4 + [
+            pltpu.VMEM((n * rows, blocks * cols), jnp.bfloat16),
+            pltpu.VMEM((blocks * cols, lanes), jnp.bfloat16),
+            pltpu.VMEM(counts.shape, jnp.float32),
+        ] + [pltpu.SemaphoreType.DMA((n, PHASES))] * 4,
+        compiler_params=pltpu.CompilerParams(
+            collective_id=0, has_side_effects=True, vmem_limit_bytes=EXCHANGE_VMEM),
+        name="exchange",
+    )(slot_block, volume, counts, *sums)
+    return pl.pallas_call(
+        finish_kernel,
         out_shape=(
             jax.ShapeDtypeStruct(volume.shape, jnp.float32),
             jax.ShapeDtypeStruct(counts.shape, jnp.bfloat16),
         ),
-        in_specs=[smem, vmem, vmem, vmem],
-        out_specs=(vmem, vmem),
-        scratch_shapes=[pltpu.VMEM(split, jnp.bfloat16)] * 4 + [
-            pltpu.VMEM((blocks * rows, lanes), jnp.bfloat16),
-            pltpu.VMEM(counts.shape, jnp.float32),
-            pltpu.VMEM((lanes, blocks * rows), jnp.float32),
-        ] + [pltpu.SemaphoreType.DMA((n, PHASES))] * 4,
-        compiler_params=pltpu.CompilerParams(collective_id=0, has_side_effects=True, vmem_limit_bytes=EXCHANGE_VMEM),
-        name="exchange",
-    )(slot_block, weights, volume, counts)
-    return updated, residual
+        in_specs=[vmem, vmem, vmem],
+        out_specs=(hbm, hbm),
+        scratch_shapes=[
+            pltpu.VMEM(volume.shape, jnp.float32),
+            pltpu.SemaphoreType.DMA((blocks + 1,)),
+        ],
+        compiler_params=pltpu.CompilerParams(vmem_limit_bytes=EXCHANGE_VMEM),
+        name="finish",
+    )(volume, gradient, residual)
 
 
 def general(tiles, volume, tile_voxel, tile_dest, slot_block, tile_count, counts):

time: 27.1 us -> 26 us (0.959)
  local copies, waits for them, and re-layouts: 1.51 us -> 0.01 us
  Pallas kernels: 24 us -> 24.4 us
    unnamed x8 -> x6, local copies, waits for them, and re-layouts: 1.51 us -> 0.01 us
    pallas_call x2 -> x3, Pallas kernels: 24 us -> 24.4 us  [the longest x1 19.3 us: fused(): pl.pallas_call(functools.partial(exchange_kernel, n), out_shape=(pltpu.VM...]
where the time goes in v3:
time: 26 us; the launch traced here: 25.8 us
  Pallas kernels  24.4 us (94%)
  between operations  1.43 us (6%)
    pallas_call x1, Pallas kernels, fused(): pl.pallas_call(functools.partial(exchange_kernel, n), out_shape=(pltpu.VM...  19.3 us
    pallas_call x1, Pallas kernels, fused(): pl.pallas_call(functools.partial(fold_kernel, blocks), out_shape=[pltpu.V...  4.18 us
    pallas_call x1, Pallas kernels, fused(): pl.pallas_call(finish_kernel, out_shape=(jax.ShapeDtypeStruct(volume.shap...  0.96 us

profile of v3, /device:TPU:0, one launch (start us, length us, event | category | flops | bytes accessed | tf_op | source)
XLA Modules:
  0.0 25.8 jit_solution(2799367595211792128)
XLA Ops:
  0.6 0.0 copy-start
  0.6 0.0 copy-start.1
  0.7 0.0 copy-start.2
  1.4 4.2 %fold_tiles.1 = (f32[64,32,128]{2,1,0:T(8,128)S(1)}, f32[64,32,128]{2,1,0:T(8,128)S(1)}, f32[64,32,128]{2,1,0:T(8,128)S(1)}, f32[64,32,128]{2,1,0:T(8,128)S(1)}) custom-call(s32[320]{0:T(512)} %dest_hbm.1, s32[320]{0:T(512)} %voxel_hbm.1, s32[1]{0:T(128)S(6)} %copy.9.count_hbm, bf16[320,128,128]{2,1,0:T(8,128)(2,1)} %tiles_ref.1), custom_call_target="tpu_custom_call" | custom-call | tf_op jit(solution)/shard_map/fold_tiles/pallas_call | solution.py:182
  5.6 0.0 copy-done
  5.6 0.0 copy-done.1
  5.6 0.0 copy-done.2
  5.6 19.3 %exchange.1 = (f32[128,1024]{1,0:T(8,128)S(1)}, bf16[8,128,128]{2,1,0:T(8,128)(2,1)S(1)}) custom-call(s32[1,8]{1,0:T(1,128)S(1)} %copy-done.2, f32[8,128,128]{2,1,0:T(8,128)S(1)} %copy-done, s32[8,128,128]{2,1,0:T(8,128)S(1)} %copy-done.1, f32[64,32,128]{2,1,0:T(8,128)S(1)} %get-tuple-element.8.refs_0_, f32[64,32,128]{2,1,0:T(8,128)S(1)} %get-tuple-element.9.refs_1_, ...), custom_call_target="tpu_custom_call" | custom-call | tf_op jit(solution)/shard_map/exchange/pallas_call | solution.py:200
  24.9 1.0 %finish.1 = (f32[8,128,128]{2,1,0:T(8,128)}, bf16[8,128,128]{2,1,0:T(8,128)(2,1)}) custom-call(f32[8,128,128]{2,1,0:T(8,128)S(1)} %copy-done, f32[128,1024]{1,0:T(8,128)S(1)} %get-tuple-element.12.grad_ref, bf16[8,128,128]{2,1,0:T(8,128)(2,1)S(1)} %get-tuple-element.13.residual_ref), custom_call_target="tpu_custom_call" | custom-call | tf_op jit(solution)/shard_map/finish/pallas_call | solution.py:217
Async XLA Ops:
  0.6 4.9 %copy-start = (f32[8,128,128]{2,1,0:T(8,128)S(1)}, f32[8,128,128]{2,1,0:T(8,128)}, u32[]{:S(2)}) copy-start(f32[8,128,128]{2,1,0:T(8,128)} %volume_ref.3) | copy-start | bytes 1572868
  0.6 4.9 %copy-start.1 = (s32[8,128,128]{2,1,0:T(8,128)S(1)}, s32[8,128,128]{2,1,0:T(8,128)}, u32[]{:S(2)}) copy-start(s32[8,128,128]{2,1,0:T(8,128)} %counts_ref.1) | copy-start | bytes 1572868
  0.7 4.9 %copy-start.2 = (s32[1,8]{1,0:T(1,128)S(1)}, s32[1,8]{1,0:T(1,128)}, u32[]{:S(2)}) copy-start(s32[1,8]{1,0:T(1,128)} %slot_ref.1) | copy-start | bytes 100

commit v4 on v3

--- a/solution.py
+++ b/solution.py
@@ -97,35 +97,35 @@
         low[v * rows:(v + 1) * rows, :] = volume_ref[v].astype(jnp.bfloat16)
 
     def project(d, p):
+        at = pl.ds(pl.multiple_of((p * n + d) * step, step), step)
         for q in range(p * step // part, (p + 1) * step // part):
-            at = pl.ds(pl.multiple_of(d * rows + q * part, part), part)
+            here = pl.ds(pl.multiple_of((p * n + d) * step + q * part - p * step, part), part)
             for v in range(blocks):
-                w_ref[at, v * rows:(v + 1) * rows] = acc[q][d * blocks + v].astype(jnp.bfloat16)
-        at = pl.ds(pl.multiple_of(d * rows + p * step, step), step)
+                w_ref[here, v * rows:(v + 1) * rows] = acc[q][d * blocks + v].astype(jnp.bfloat16)
         return jnp.dot(w_ref[at, :], low[...], preferred_element_type=jnp.float32).astype(jnp.bfloat16)
 
     def send(src, dst, send_sems, recv_sems, peer, p):
         return pltpu.make_async_remote_copy(
-            src_ref=src.at[peer, p], dst_ref=dst.at[me, p],
+            src_ref=src.at[p, peer], dst_ref=dst.at[p, me],
             send_sem=send_sems.at[peer, p], recv_sem=recv_sems.at[me, p],
             device_id={"dom": peer}, device_id_type=pl.DeviceIdType.MESH)
 
     def arrival(dst, send_sems, recv_sems, peer, p):
         return pltpu.make_async_remote_copy(
-            src_ref=dst.at[peer, p], dst_ref=dst.at[peer, p],
+            src_ref=dst.at[p, peer], dst_ref=dst.at[p, peer],
             send_sem=send_sems.at[peer, p], recv_sem=recv_sems.at[peer, p],
             device_id={"dom": peer}, device_id_type=pl.DeviceIdType.MESH)
 
     first = True
     for p in range(PHASES):
         for peer in order:
-            out_buf[peer, p] = project(peer, p)
+            out_buf[p, peer] = project(peer, p)
             if first:
                 pl.semaphore_wait(barrier, n - 1)
                 first = False
             send(out_buf, in_buf, out_send, out_recv, peer, p).start()
     for p in range(PHASES):
-        in_buf[me, p] = project(me, p)
+        in_buf[p, me] = project(me, p)
     for b in range(owned):
         measured[b] = jnp.log(flux / counts_ref[b].astype(jnp.float32))
 
@@ -136,23 +136,32 @@
         for b in range(owned):
             total = jnp.zeros((step, lanes), jnp.float32)
             for s in range(n):
-                total += jnp.where(slot_ref[0, s] == b, in_buf[s, p].astype(jnp.float32), 0.0)
+                total += jnp.where(slot_ref[0, s] == b, in_buf[p, s].astype(jnp.float32), 0.0)
             residual_ref[b, at, :] = (total - measured[b, at, :]).astype(jnp.bfloat16)
         for peer in order:
-            answer_buf[peer, p] = residual_ref[slot_ref[0, peer], at, :]
+            answer_buf[p, peer] = residual_ref[slot_ref[0, peer], at, :]
             send(answer_buf, landing, back_send, back_recv, peer, p).start()
-        landing[me, p] = residual_ref[slot_ref[0, me], at, :]
-
-    def pull(d):
-        held = landing[d].reshape(rows, lanes)
-        at = pl.ds(pl.multiple_of(d * rows, rows), rows)
+        landing[p, me] = residual_ref[slot_ref[0, me], at, :]
+
+    half = n // 2
+    near = me // half
+    mine = [near * half + (me + j) % half for j in range(1, half)]
+    theirs = [(1 - near) * half + j for j in range(half)]
+
+    def pull(p, side):
+        start = pl.multiple_of(side * half, half)
+        held = landing[p, pl.ds(start, half)].reshape(half * step, lanes)
+        at = pl.ds(pl.multiple_of((p * n + start) * step, half * step), half * step)
         return jnp.dot(held.T, w_ref[at, :], preferred_element_type=jnp.float32)
 
-    grad_ref[...] = pull(me)
-    for peer in reversed(order):
-        for p in range(PHASES):
-            arrival(landing, back_send, back_recv, peer, p).wait_recv()
-        grad_ref[...] += pull(peer)
+    for p in range(PHASES):
+        for side, peers in ((near, mine), (1 - near, theirs)):
+            for peer in peers:
+                arrival(landing, back_send, back_recv, peer, p).wait_recv()
+            if p == 0 and peers is mine:
+                grad_ref[...] = pull(p, side)
+            else:
+                grad_ref[...] += pull(p, side)
     for p in range(PHASES):
         for peer in order:
             send(out_buf, in_buf, out_send, out_recv, peer, p).wait_send()
@@ -196,7 +205,7 @@
         name="fold_tiles",
     )(tile_dest, tile_voxel, tile_count, tiles)
 
-    split = (n, PHASES, rows // PHASES, lanes)
+    split = (PHASES, n, rows // PHASES, lanes)
     gradient, residual = pl.pallas_call(
         functools.partial(exchange_kernel, n),
         out_shape=(

time: 26 us -> 25.9 us (level)
  no operation moved by 1% of the time
where the time goes in v4:
time: 25.9 us; the launch traced here: 25.7 us
  Pallas kernels  24.3 us (94%)
  between operations  1.43 us (6%)
    pallas_call x1, Pallas kernels, fused(): pl.pallas_call(functools.partial(exchange_kernel, n), out_shape=(pltpu.VM...  19.1 us
    pallas_call x1, Pallas kernels, fused(): pl.pallas_call(functools.partial(fold_kernel, blocks), out_shape=[pltpu.V...  4.18 us
    pallas_call x1, Pallas kernels, fused(): pl.pallas_call(finish_kernel, out_shape=(jax.ShapeDtypeStruct(volume.shap...  0.96 us

profile of v4, /device:TPU:0, one launch (start us, length us, event | category | flops | bytes accessed | tf_op | source)
XLA Modules:
  0.0 25.7 jit_solution(2453193315839831700)
XLA Ops:
  0.6 0.0 copy-start
  0.6 0.0 copy-start.1
  0.7 0.0 copy-start.2
  1.4 4.2 %fold_tiles.1 = (f32[64,32,128]{2,1,0:T(8,128)S(1)}, f32[64,32,128]{2,1,0:T(8,128)S(1)}, f32[64,32,128]{2,1,0:T(8,128)S(1)}, f32[64,32,128]{2,1,0:T(8,128)S(1)}) custom-call(s32[320]{0:T(512)} %dest_hbm.1, s32[320]{0:T(512)} %voxel_hbm.1, s32[1]{0:T(128)S(6)} %copy.9.count_hbm, bf16[320,128,128]{2,1,0:T(8,128)(2,1)} %tiles_ref.1), custom_call_target="tpu_custom_call" | custom-call | tf_op jit(solution)/shard_map/fold_tiles/pallas_call | solution.py:191
  5.6 0.0 copy-done
  5.6 0.0 copy-done.1
  5.6 0.0 copy-done.2
  5.6 19.1 %exchange.1 = (f32[128,1024]{1,0:T(8,128)S(1)}, bf16[8,128,128]{2,1,0:T(8,128)(2,1)S(1)}) custom-call(s32[1,8]{1,0:T(1,128)S(1)} %copy-done.2, f32[8,128,128]{2,1,0:T(8,128)S(1)} %copy-done, s32[8,128,128]{2,1,0:T(8,128)S(1)} %copy-done.1, f32[64,32,128]{2,1,0:T(8,128)S(1)} %get-tuple-element.8.refs_0_, f32[64,32,128]{2,1,0:T(8,128)S(1)} %get-tuple-element.9.refs_1_, ...), custom_call_target="tpu_custom_call" | custom-call | tf_op jit(solution)/shard_map/exchange/pallas_call | solution.py:209
  24.7 1.0 %finish.1 = (f32[8,128,128]{2,1,0:T(8,128)}, bf16[8,128,128]{2,1,0:T(8,128)(2,1)}) custom-call(f32[8,128,128]{2,1,0:T(8,128)S(1)} %copy-done, f32[128,1024]{1,0:T(8,128)S(1)} %get-tuple-element.12.grad_ref, bf16[8,128,128]{2,1,0:T(8,128)(2,1)S(1)} %get-tuple-element.13.residual_ref), custom_call_target="tpu_custom_call" | custom-call | tf_op jit(solution)/shard_map/finish/pallas_call | solution.py:226
Async XLA Ops:
  0.6 4.9 %copy-start = (f32[8,128,128]{2,1,0:T(8,128)S(1)}, f32[8,128,128]{2,1,0:T(8,128)}, u32[]{:S(2)}) copy-start(f32[8,128,128]{2,1,0:T(8,128)} %volume_ref.3) | copy-start | bytes 1572868
  0.6 4.9 %copy-start.1 = (s32[8,128,128]{2,1,0:T(8,128)S(1)}, s32[8,128,128]{2,1,0:T(8,128)}, u32[]{:S(2)}) copy-start(s32[8,128,128]{2,1,0:T(8,128)} %counts_ref.1) | copy-start | bytes 1572868
  0.7 4.9 %copy-start.2 = (s32[1,8]{1,0:T(1,128)S(1)}, s32[1,8]{1,0:T(1,128)}, u32[]{:S(2)}) copy-start(s32[1,8]{1,0:T(1,128)} %slot_ref.1) | copy-start | bytes 100

commit v5 on v4

--- a/solution.py
+++ b/solution.py
@@ -9,7 +9,7 @@
 
 flux = 32768.0
 step_size = 0.5
-GROUP = 16
+GROUP = 32
 PARTS = 4
 PHASES = 2
 FOLD_VMEM = 53 * 1024 * 1024

time: 25.9 us -> 25.8 us (level)
  no operation moved by 1% of the time
where the time goes in v5:
time: 25.8 us; the launch traced here: 25.6 us
  Pallas kernels  24.2 us (94%)
  between operations  1.43 us (6%)
    pallas_call x1, Pallas kernels, fused(): pl.pallas_call(functools.partial(exchange_kernel, n), out_shape=(pltpu.VM...  19.1 us
    pallas_call x1, Pallas kernels, fused(): pl.pallas_call(functools.partial(fold_kernel, blocks), out_shape=[pltpu.V...  4.12 us
    pallas_call x1, Pallas kernels, fused(): pl.pallas_call(finish_kernel, out_shape=(jax.ShapeDtypeStruct(volume.shap...  0.96 us

profile of v5, /device:TPU:0, one launch (start us, length us, event | category | flops | bytes accessed | tf_op | source)
XLA Modules:
  0.0 25.6 jit_solution(11342724264705171827)
XLA Ops:
  0.6 0.0 copy-start
  0.6 0.0 copy-start.1
  0.7 0.0 copy-start.2
  1.4 4.1 %fold_tiles.1 = (f32[64,32,128]{2,1,0:T(8,128)S(1)}, f32[64,32,128]{2,1,0:T(8,128)S(1)}, f32[64,32,128]{2,1,0:T(8,128)S(1)}, f32[64,32,128]{2,1,0:T(8,128)S(1)}) custom-call(s32[320]{0:T(512)} %dest_hbm.1, s32[320]{0:T(512)} %voxel_hbm.1, s32[1]{0:T(128)S(6)} %copy.9.count_hbm, bf16[320,128,128]{2,1,0:T(8,128)(2,1)} %tiles_ref.1), custom_call_target="tpu_custom_call" | custom-call | tf_op jit(solution)/shard_map/fold_tiles/pallas_call | solution.py:191
  5.5 0.0 copy-done
  5.5 0.0 copy-done.1
  5.5 0.0 copy-done.2
  5.5 19.1 %exchange.1 = (f32[128,1024]{1,0:T(8,128)S(1)}, bf16[8,128,128]{2,1,0:T(8,128)(2,1)S(1)}) custom-call(s32[1,8]{1,0:T(1,128)S(1)} %copy-done.2, f32[8,128,128]{2,1,0:T(8,128)S(1)} %copy-done, s32[8,128,128]{2,1,0:T(8,128)S(1)} %copy-done.1, f32[64,32,128]{2,1,0:T(8,128)S(1)} %get-tuple-element.8.refs_0_, f32[64,32,128]{2,1,0:T(8,128)S(1)} %get-tuple-element.9.refs_1_, ...), custom_call_target="tpu_custom_call" | custom-call | tf_op jit(solution)/shard_map/exchange/pallas_call | solution.py:209
  24.7 1.0 %finish.1 = (f32[8,128,128]{2,1,0:T(8,128)}, bf16[8,128,128]{2,1,0:T(8,128)(2,1)}) custom-call(f32[8,128,128]{2,1,0:T(8,128)S(1)} %copy-done, f32[128,1024]{1,0:T(8,128)S(1)} %get-tuple-element.12.grad_ref, bf16[8,128,128]{2,1,0:T(8,128)(2,1)S(1)} %get-tuple-element.13.residual_ref), custom_call_target="tpu_custom_call" | custom-call | tf_op jit(solution)/shard_map/finish/pallas_call | solution.py:226
Async XLA Ops:
  0.6 4.9 %copy-start = (f32[8,128,128]{2,1,0:T(8,128)S(1)}, f32[8,128,128]{2,1,0:T(8,128)}, u32[]{:S(2)}) copy-start(f32[8,128,128]{2,1,0:T(8,128)} %volume_ref.3) | copy-start | bytes 1572868
  0.6 4.9 %copy-start.1 = (s32[8,128,128]{2,1,0:T(8,128)S(1)}, s32[8,128,128]{2,1,0:T(8,128)}, u32[]{:S(2)}) copy-start(s32[8,128,128]{2,1,0:T(8,128)} %counts_ref.1) | copy-start | bytes 1572868
  0.7 4.9 %copy-start.2 = (s32[1,8]{1,0:T(1,128)S(1)}, s32[1,8]{1,0:T(1,128)}, u32[]{:S(2)}) copy-start(s32[1,8]{1,0:T(1,128)} %slot_ref.1) | copy-start | bytes 100
